TPU v7x, 256 devices: a whole 4x4x8 slice. The times are simulated.
256 devices in a mesh: role: 2 (over core), dev: 64 (over x_hi, y, z), head: 2 (over x_lo).
Axes of the slice: x: 4 (x_hi: 2, x_lo: 2; x = x_hi * 2 + x_lo), y: 4, z: 8, core: 2. Of those that a mesh axis runs over, the one named last changes fastest.
Arguments:
- hidden: bfloat16 [2048, 4096], P(('role', 'dev', 'head')), may hold values from -6 to 6
- queries: bfloat16 [2048, 64, 128], P(('role', 'dev'), 'head'), as said below
- cache_keys: bfloat16 [2048, 128, 4, 128], P(('role', 'dev'), None, 'head'), as said below
- cache_values: bfloat16 [2048, 128, 4, 128], P(('role', 'dev'), None, 'head'), may hold values from -6 to 6
- new_keys: bfloat16 [2048, 4, 128], P(('role', 'dev'), 'head'), may hold values from -6 to 6
- new_values: bfloat16 [2048, 4, 128], P(('role', 'dev'), 'head'), may hold values from -6 to 6
- lengths: int32 [2048], P(('role', 'dev')), may hold values from 32 to 128, as said below
- out_proj: bfloat16 [8192, 4096], P('head', 'dev'), may hold values from -0.5 to 0.5
- norm_gain: float32 [4096], replicated, may hold values from 0.1 to 1.9
- expert_gate: bfloat16 [128, 4096, 768], P(('role', 'dev'), None, 'head'), may hold values from -0.09375 to 0.09375
- expert_up: bfloat16 [128, 4096, 768], P(('role', 'dev'), None, 'head'), may hold values from -0.09375 to 0.09375
- expert_down: bfloat16 [128, 768, 4096], P(('role', 'dev'), 'head'), may hold values from -0.21875 to 0.21875
- expert_ids: int32 [2048, 8], P(('role', 'dev', 'head')), may hold values from 0 to 127, all different within a row; in each aligned block of 8 rows (0 to 7, 8 to 15, ...) at most 2 rows name the same one
- gate_levels: int32 [2048, 8], P(('role', 'dev', 'head')), may hold values from 1 to 255
Outputs:
- layer_out: bfloat16 [2048, 4096], P(('role', 'dev', 'head'))
Inputs may be any that keep to these rules, and one draw needn't show every extreme that they name: `queries`: query vectors of the new tokens. `cache_keys`: cached keys of the requests. `lengths`: the first request of each block of 16 rows holds 128 positions and the second holds 32. `expert_ids`: each row names 8 different experts; among the 8 rows of one device no expert is named more than 2 times, a bound that some block reaches.
All inputs are finite; a program needn't handle non-finite values.
Results may differ from a plain program's by a relative error of at most 0.0065.
Values may be sent and summed in bfloat16 or wider, within the bound.
No kernel may reach another device: no remote copies, remote signals or barrier semaphores. Data moves between devices by JAX's collectives and lax.ppermute only.
A program may use at most 64 MiB of HBM per device.

v0:
```python
import math
import jax
import jax.numpy as jnp
from jax import lax
from jax.sharding import PartitionSpec as P


def attend_block(query_rows, key_rows, value_rows, key_new, value_new, valid_len):
    row_count = query_rows.shape[0]
    kv_heads = key_rows.shape[2]
    group_size = query_rows.shape[1] // kv_heads
    head_dim = query_rows.shape[2]
    scaling = 1.0 / math.sqrt(head_dim)
    query_f = query_rows.astype(jnp.float32).reshape(row_count, kv_heads, group_size, head_dim)
    scores = jnp.einsum("bhgd,bthd->bhgt", query_f, key_rows.astype(jnp.float32)) * scaling
    scores_new = jnp.einsum("bhgd,bhd->bhg", query_f, key_new.astype(jnp.float32)) * scaling
    positions = jnp.arange(key_rows.shape[1], dtype=jnp.int32)
    usable = (positions[None, :] < valid_len[:, None])[:, None, None, :]
    masked = jnp.where(usable, scores, -1e30)
    highest = jnp.maximum(jnp.max(masked, axis=-1), scores_new)
    exp_terms = jnp.exp(masked - highest[..., None])
    exp_new = jnp.exp(scores_new - highest)
    totals = jnp.sum(exp_terms, axis=-1) + exp_new
    weights = (exp_terms / totals[..., None]).astype(jnp.bfloat16)
    weight_new = (exp_new / totals).astype(jnp.bfloat16)
    blended = jnp.einsum("bhgt,bthd->bhgd", weights, value_rows, preferred_element_type=jnp.float32)
    blended = (
        blended
        + weight_new.astype(jnp.float32)[..., None] * value_new.astype(jnp.float32)[:, :, None, :]
    )
    return blended.astype(jnp.bfloat16).reshape(row_count, kv_heads * group_size * head_dim)


def expert_rows(rows_in, gate_w, up_w, down_w):
    gate_part = jnp.dot(rows_in, gate_w, preferred_element_type=jnp.float32)
    up_part = jnp.dot(rows_in, up_w, preferred_element_type=jnp.float32)
    active = (jax.nn.silu(gate_part) * up_part).astype(jnp.bfloat16)
    return jnp.dot(active, down_w, preferred_element_type=jnp.float32)


def slot_ranks(flat_ids, experts):
    one_hot = (flat_ids[:, None] == jnp.arange(experts, dtype=jnp.int32)[None, :]).astype(jnp.int32)
    return jnp.sum(jnp.cumsum(one_hot, axis=0) * one_hot, axis=1) - 1


def on_device(
    hidden,
    queries,
    cache_keys,
    cache_values,
    new_keys,
    new_values,
    lengths,
    out_proj,
    norm_gain,
    expert_gate,
    expert_up,
    expert_down,
    expert_ids,
    gate_levels,
):
    attended = attend_block(queries, cache_keys, cache_values, new_keys, new_values, lengths)
    columns = jnp.dot(
        lax.all_gather(attended, "dev", axis=0, tiled=True),
        out_proj,
        preferred_element_type=jnp.float32,
    )
    dev_count = lax.axis_size("dev")
    head_count = lax.axis_size("head")
    experts = lax.axis_size("role") * dev_count
    col_width = out_proj.shape[1]
    width = dev_count * col_width
    projected = lax.all_to_all(columns, ("dev", "head"), split_axis=0, concat_axis=1, tiled=True)
    tokens = projected.shape[0]
    summed = jnp.sum(projected.reshape(tokens, dev_count, head_count, col_width), axis=2).reshape(
        tokens, width
    )
    residual = hidden.astype(jnp.float32) + summed
    normed = (
        residual
        * lax.rsqrt(jnp.mean(residual * residual, axis=-1, keepdims=True) + 1e-06)
        * norm_gain
    ).astype(jnp.bfloat16)
    top_k = expert_ids.shape[1]
    capacity = max(2, 2 * tokens * top_k // experts)
    own_ids = expert_ids.reshape(-1)
    own_ranks = slot_ranks(own_ids, experts)
    pair_rows, pair_ids = (
        lax.all_gather(normed, "head", axis=0, tiled=True),
        lax.all_gather(expert_ids, "head", axis=0, tiled=True),
    )
    pair_flat = pair_ids.reshape(head_count, tokens * top_k)
    pair_ranks = jax.vmap(lambda id_row: slot_ranks(id_row, experts))(pair_flat)
    pair_ranks = pair_ranks + capacity * jnp.arange(head_count, dtype=jnp.int32)[:, None]
    rows_from = jnp.arange(head_count * tokens * top_k, dtype=jnp.int32) // top_k
    outgoing = (
        jnp.zeros((experts, head_count * capacity, width), jnp.bfloat16)
        .at[pair_flat.reshape(-1), pair_ranks.reshape(-1)]
        .set(pair_rows[rows_from])
    )
    incoming = lax.all_to_all(outgoing, ("role", "dev"), split_axis=0, concat_axis=0, tiled=True)
    sources = incoming.shape[0]
    slot_total = incoming.shape[1]
    partial_value = expert_rows(
        incoming.reshape(sources * slot_total, width), expert_gate[0], expert_up[0], expert_down[0]
    )
    partial_value = partial_value.reshape(sources, slot_total, width).astype(jnp.bfloat16)
    arrived = lax.all_to_all(
        partial_value, ("role", "dev"), split_axis=0, concat_axis=0, tiled=True
    )
    arrived = (
        lax.psum_scatter(arrived, "head", scatter_dimension=1, tiled=True)
        .astype(jnp.float32)
        .astype(jnp.bfloat16)
    )
    picked = arrived[own_ids, own_ranks].astype(jnp.float32).reshape(tokens, top_k, width)
    levels = gate_levels.astype(jnp.float32)
    shares = levels / jnp.sum(levels, axis=1, keepdims=True)
    return (residual + jnp.sum(shares[..., None] * picked, axis=1)).astype(jnp.bfloat16)


def solution(mesh):
    placed = (
        P(("role", "dev", "head"), None),
        P(("role", "dev"), "head", None),
        P(("role", "dev"), None, "head", None),
        P(("role", "dev"), None, "head", None),
        P(("role", "dev"), "head", None),
        P(("role", "dev"), "head", None),
        P(("role", "dev")),
        P("head", "dev"),
        P(),
        P(("role", "dev"), None, "head"),
        P(("role", "dev"), None, "head"),
        P(("role", "dev"), "head", None),
        P(("role", "dev", "head"), None),
        P(("role", "dev", "head"), None),
    )
    return jax.shard_map(
        on_device,
        mesh=mesh,
        in_specs=placed,
        out_specs=P(("role", "dev", "head"), None),
        check_vma=False,
    )
```

profile of v0, /device:TPU:1, one launch (start us, length us, event | category | flops | bytes accessed | tf_op | source)
XLA Modules:
  0.0 560.9 jit_solution(16563779175409254275)
XLA Ops:
  6.5 0.9 iota_compare_fusion.2
  7.4 1.1 fusion.22
  8.6 2.1 fusion.34
  11.7 1.7 fusion.12
  14.1 3.7 all_gather.10
  18.3 148.0 %all-gather.2.cloned.1.call-done = bf16[1024,4096]{1,0:T(8,128)(2,1)} async-done(((bf16[16,4096]{1,0:T(8,128)(2,1)}), bf16[1024,4096]{1,0:T(8,128)(2,1)}) %all-gather.2.cloned.1.call-update) | async-done | bytes 8388624 | tf_op jit(solution)/shard_map/all_gather | solution.py:64
  166.3 6.6 %convolution_bitcast_fusion = f32[128,8,64]{2,1,0:T(8,128)} fusion(bf16[1024,4096]{1,0:T(8,128)(2,1)} %all-gather.2.cloned.1.call-done, bf16[4096,64]{0,1:T(8,128)(2,1)} %param.21), kind=kOutput, calls=%fused_computation.11 | convolution fusion | flops 536870912 | bytes 9175040 | tf_op jit(solution)/shard_map/dot_general | solution.py:63
  172.9 2.1 reshape.251
  175.0 9.4 %all-to-all-start = ((f32[128,1,512]{2,1,0:T(1,128)}), f32[128,1,512]{2,1,0:T(1,128)S(1)}, u32[]{:S(2)}, u32[]{:S(2)}) async-start(f32[128,1,512]{2,1,0:T(1,128)} %reshape.251), calls=%async_computation | async-start | bytes 524288 | tf_op jit(solution)/shard_map/all_to_all | solution.py:73
  184.8 11.2 %all-to-all-done = f32[128,1,512]{2,1,0:T(1,128)S(1)} async-done(((f32[128,1,512]{2,1,0:T(1,128)}), f32[128,1,512]{2,1,0:T(1,128)S(1)}, u32[]{:S(2)}, u32[]{:S(2)}) %all-to-all-start) | async-done | bytes 262176 | tf_op jit(solution)/shard_map/all_to_all | solution.py:73
  197.2 2.2 reduce
  199.5 0.9 reshape.252
  200.4 1.1 bitcast_reduce_fusion
  201.5 0.7 copy.33
  202.3 1.1 reshape.224
  203.6 3.8 all_gather.11
  207.4 2.2 gather_fusion
  209.5 4.0 broadcast_in_dim.16
  213.6 32.4 %scatter_fusion = bf16[128,4,4096]{2,1,0:T(4,128)(2,1)} fusion(bf16[128,4,4096]{2,1,0:T(4,128)(2,1)} %broadcast_in_dim.16, s32[128]{0:T(128)S(1)} %fusion.32, bf16[128,4096]{1,0:T(8,128)(2,1)} %gather_fusion), kind=kCustom, calls=%fused_computation.2 | custom fusion | bytes 3146752 | tf_op jit(solution)/shard_map/scatter | solution.py:99
  246.0 112.3 %all_to_all.26 = bf16[128,4,4096]{2,1,0:T(4,128)(2,1)} all-to-all(bf16[128,4,4096]{2,1,0:T(4,128)(2,1)} %scatter_fusion), channel_id=1, replica_groups=mesh['role'=2,'dev'=64,'head'=2] {'role','dev'}, dimensions={0} | all-to-all | bytes 8388608 | tf_op jit(solution)/shard_map/all_to_all | solution.py:101
  358.3 6.9 %reshape.225 = bf16[512,4096]{1,0:T(8,128)(2,1)} reshape(bf16[128,4,4096]{2,1,0:T(4,128)(2,1)} %all_to_all.26) | data formatting | bytes 8388608 | tf_op jit(solution)/shard_map/reshape | solution.py:105
  365.2 5.6 %fusion.3 = f32[512,384]{1,0:T(8,128)S(1)} fusion(bf16[512,4096]{1,0:T(8,128)(2,1)} %reshape.225, bf16[1,4096,384]{2,1,0:T(8,128)(2,1)} %param.23), kind=kOutput, calls=%fused_computation.7 | convolution fusion | flops 1610612736 | bytes 8126464 | tf_op jit(solution)/shard_map/dot_general | solution.py:35
  370.8 3.1 fusion.8
  373.9 1.8 dot_general.29
  375.8 3.3 convolution_convert_fusion
  379.1 3.2 copy.35
  382.3 104.9 %all_to_all.27 = bf16[128,4,4096]{2,1,0:T(4,128)(2,1)S(1)} all-to-all(bf16[128,4,4096]{2,1,0:T(4,128)(2,1)S(1)} %copy.35), channel_id=1, replica_groups=mesh['role'=2,'dev'=64,'head'=2] {'role','dev'}, dimensions={0} | all-to-all | bytes 8388608 | tf_op jit(solution)/shard_map/all_to_all | solution.py:108
  487.3 4.2 copy.36
  492.6 50.9 %reduce-scatter.2.cloned.1.call-done = bf16[128,2,4096]{2,0,1:T(8,128)(2,1)} async-done(((bf16[128,4,4096]{2,0,1:T(8,128)(2,1)}), bf16[128,2,4096]{2,0,1:T(8,128)(2,1)}) %reduce-scatter.2.cloned.1.call-update) | async-done | bytes 2097168 | tf_op jit(solution)/shard_map/reduce_scatter | solution.py:112
  543.5 5.1 copy.37
  548.6 3.3 gather_fusion.1
  551.9 1.5 fusion.13
  (49 shorter events, 5.7 us)
Async XLA Ops:
  6.5 369.2 %copy-start = (bf16[1,384,4096]{2,1,0:T(8,128)(2,1)S(1)}, bf16[1,384,4096]{2,1,0:T(8,128)(2,1)}, u32[]{:S(2)}) copy-start(bf16[1,384,4096]{2,1,0:T(8,128)(2,1)} %param.25) | copy-start | bytes 9437188
  6.5 7.6 %copy-start.4 = (s32[8,8]{1,0:T(8,128)S(1)}, s32[8,8]{1,0:T(8,128)}, u32[]{:S(2)}) copy-start(s32[8,8]{1,0:T(8,128)} %param.26) | copy-start | bytes 772
  6.5 159.8 %all-gather.2.cloned.1.call-start = ((), (), s32[]{:S(2)}) async-start(), calls=%async_computation.4 | async-start | bytes 8519680 | tf_op jit(solution)/shard_map/all_gather | solution.py:64
  172.9 30.4 %copy-start.3 = (bf16[8,4096]{1,0:T(8,128)(2,1)S(1)}, bf16[8,4096]{1,0:T(8,128)(2,1)}, u32[]{:S(2)}) copy-start(bf16[8,4096]{1,0:T(8,128)(2,1)} %param.14) | copy-start | bytes 196612
  172.9 30.6 %copy-start.5 = (f32[4096]{0:T(1024)S(1)}, f32[4096]{0:T(1024)}, u32[]{:S(2)}) copy-start(f32[4096]{0:T(1024)} %param.22) | copy-start | bytes 49156
  175.0 21.0 %all-to-all-start = ((f32[128,1,512]{2,1,0:T(1,128)}), f32[128,1,512]{2,1,0:T(1,128)S(1)}, u32[]{:S(2)}, u32[]{:S(2)}) async-start(f32[128,1,512]{2,1,0:T(1,128)} %reshape.251), calls=%async_computation | async-start | bytes 524288 | tf_op jit(solution)/shard_map/all_to_all | solution.py:73
  184.5 359.0 %reduce-scatter.2.cloned.1.call-start = ((), (), s32[]{:S(2)}) async-start(), calls=%async_computation.5 | async-start | bytes 6291456 | tf_op jit(solution)/shard_map/reduce_scatter | solution.py:112
  196.0 0.7 copy-start.2
  365.2 5.6 %copy-start.1 = (bf16[512,4096]{1,0:T(8,128)(2,1)S(1)}, bf16[512,4096]{1,0:T(8,128)(2,1)}, u32[]{:S(2)}) copy-start(bf16[512,4096]{1,0:T(8,128)(2,1)} %reshape.225) | copy-start | bytes 12582916
  365.2 5.6 %copy-start.7 = (bf16[1,4096,384]{2,1,0:T(8,128)(2,1)S(1)}, bf16[1,4096,384]{2,1,0:T(8,128)(2,1)}, u32[]{:S(2)}) copy-start(bf16[1,4096,384]{2,1,0:T(8,128)(2,1)} %param.24) | copy-start | bytes 9437188
  491.5 0.7 copy-start.6
Sparse Core Ops, SparseCore 0:
  14.3 152.0 all-gather.1
  491.6 51.7 reduce-scatter.1
where the time goes:
time: 562 us; the launch traced here: 561 us
  blocking collectives  225 us (40%)
  waiting for transfers between devices  210 us (37%)
  local copies, waits for them, and re-layouts  70.8 us (13%)
  matrix products  23.5 us (4%)
  between operations  13.6 us (2%)
  starting transfers between devices  9.48 us (2%)
  other arithmetic  8.69 us (2%)
    all_gather x1, waiting for transfers between devices, on_device(): lax.all_gather(attended, 'dev', axis=0, tiled=True)  148 us
    all_to_all x1, blocking collectives, on_device(): lax.all_to_all(outgoing, ('role', 'dev'), split_axis=0, concat_axis=0, ti...  112 us
    all_to_all x1, blocking collectives, on_device(): lax.all_to_all(partial_value, ('role', 'dev'), split_axis=0, concat_axis=...  105 us
    reduce_scatter x1, waiting for transfers between devices, on_device(): lax.psum_scatter(arrived, 'head', scatter_dimension=1, tiled=True)  50.9 us
    scatter x1, local copies, waits for them, and re-layouts, on_device(): outgoing = jnp.zeros((experts, head_count * capacity, width), jnp.bfloat1...  32.4 us
  transfers between devices with their start and end apart: 3, of which 3 were waited for; matrix products, arithmetic and copies ran while one was open for 0% of the time, Pallas kernels for 0%

commit v1 on v0

--- a/solution.py
+++ b/solution.py
@@ -3,6 +3,13 @@
 import jax.numpy as jnp
 from jax import lax
 from jax.sharding import PartitionSpec as P
+
+
+def gather_over(x, name, dim):
+    devices = lax.axis_size(name)
+    blocks = jnp.stack([x for _ in range(devices)])
+    blocks = lax.all_to_all(blocks, name, split_axis=0, concat_axis=0)
+    return jnp.concatenate(blocks, axis=dim)
 
 
 def attend_block(query_rows, key_rows, value_rows, key_new, value_new, valid_len):
@@ -60,11 +67,7 @@
     gate_levels,
 ):
     attended = attend_block(queries, cache_keys, cache_values, new_keys, new_values, lengths)
-    columns = jnp.dot(
-        lax.all_gather(attended, "dev", axis=0, tiled=True),
-        out_proj,
-        preferred_element_type=jnp.float32,
-    )
+    columns = jnp.dot(gather_over(attended, "dev", 0), out_proj, preferred_element_type=jnp.float32)
     dev_count = lax.axis_size("dev")
     head_count = lax.axis_size("head")
     experts = lax.axis_size("role") * dev_count

time: 562 us -> 615 us (1.094)
  starting transfers between devices: 9.48 us -> 29.4 us
  blocking collectives: 225 us -> 241 us
  waiting for transfers between devices: 210 us -> 223 us
    all_to_all x0 -> x1, waiting for transfers between devices: none -> 161 us  [gather_over(): blocks = lax.all_to_all(blocks, name, split_axis=0, concat_axis=0)]
    all_gather x1 -> x0, waiting for transfers between devices: 148 us -> none  [on_device(): lax.all_gather(attended, 'dev', axis=0, tiled=True)]
    all_gather x1, blocking collectives: 3.74 us -> 21.4 us  [on_device(): lax.all_gather(expert_ids, 'head', axis=0, tiled=True)]
    all_to_all x0 -> x1, starting transfers between devices: none -> 15.5 us  [gather_over(): blocks = lax.all_to_all(blocks, name, split_axis=0, concat_axis=0)]
where the time goes in v1:
time: 615 us; the launch traced here: 614 us
  blocking collectives  241 us (39%)
  waiting for transfers between devices  223 us (36%)
  local copies, waits for them, and re-layouts  74.4 us (12%)
  starting transfers between devices  29.4 us (5%)
  matrix products  23.5 us (4%)
  between operations  13.6 us (2%)
  other arithmetic  8.69 us (1%)
    all_to_all x1, waiting for transfers between devices, gather_over(): blocks = lax.all_to_all(blocks, name, split_axis=0, concat_axis=0)  161 us
    all_to_all x1, blocking collectives, on_device(): lax.all_to_all(outgoing, ('role', 'dev'), split_axis=0, concat_axis=0, ti...  111 us
    all_to_all x1, blocking collectives, on_device(): lax.all_to_all(partial_value, ('role', 'dev'), split_axis=0, concat_axis=...  105 us
    reduce_scatter x1, waiting for transfers between devices, on_device(): lax.psum_scatter(arrived, 'head', scatter_dimension=1, tiled=True)  50.9 us
    scatter x1, local copies, waits for them, and re-layouts, on_device(): outgoing = jnp.zeros((experts, head_count * capacity, width), jnp.bfloat1...  32.4 us
    all_gather x1, blocking collectives, on_device(): lax.all_gather(expert_ids, 'head', axis=0, tiled=True)  21.4 us
    all_to_all x1, starting transfers between devices, gather_over(): blocks = lax.all_to_all(blocks, name, split_axis=0, concat_axis=0)  15.5 us
    all_to_all x1, starting transfers between devices, on_device(): lax.all_to_all(columns, ('dev', 'head'), split_axis=0, concat_axis=1, til...  13.9 us
  transfers between devices with their start and end apart: 3, of which 3 were waited for; matrix products, arithmetic and copies ran while one was open for 0% of the time, Pallas kernels for 0%

profile of v1, /device:TPU:1, one launch (start us, length us, event | category | flops | bytes accessed | tf_op | source)
XLA Modules:
  0.0 613.8 jit_solution(7271716496908145338)
XLA Ops:
  7.4 1.1 fusion.24
  8.6 2.1 fusion.36
  11.7 1.7 fusion.12
  13.4 4.3 stack.3
  17.7 15.5 %all-to-all-start = ((bf16[64,16,4096]{2,1,0:T(8,128)(2,1)}), bf16[64,16,4096]{2,1,0:T(8,128)(2,1)}, u32[]{:S(2)}, u32[]{:S(2)}) async-start(bf16[64,16,4096]{2,1,0:T(8,128)(2,1)} %stack.3), calls=%async_computation | async-start | bytes 16777216 | tf_op jit(solution)/shard_map/all_to_all | solution.py:11
  33.2 21.4 %all_gather.6 = s32[16,8]{1,0:T(8,128)S(1)} all-gather(s32[8,8]{1,0:T(8,128)S(1)} %copy-done.5), channel_id=1, replica_groups=mesh['role'=2,'dev'=64,'head'=2] {'head'}, dimensions={0}, use_global_device_ids=true | all-gather | bytes 768 | tf_op jit(solution)/shard_map/all_gather | solution.py:93
  55.1 160.8 %all-to-all-done = bf16[64,16,4096]{2,1,0:T(8,128)(2,1)} async-done(((bf16[64,16,4096]{2,1,0:T(8,128)(2,1)}), bf16[64,16,4096]{2,1,0:T(8,128)(2,1)}, u32[]{:S(2)}, u32[]{:S(2)}) %all-to-all-start) | async-done | bytes 8388640 | tf_op jit(solution)/shard_map/all_to_all | solution.py:11
  215.9 6.6 %fusion.16 = f32[128,8,64]{2,1,0:T(8,128)} fusion(bf16[128,8,4096]{2,1,0:T(8,128)(2,1)} %bitcast.4, bf16[4096,64]{0,1:T(8,128)(2,1)} %param.21), kind=kOutput, calls=%fused_computation.20 | convolution fusion | flops 536870912 | bytes 9175040 | tf_op jit(solution)/shard_map/dot_general | solution.py:70
  222.5 2.1 reshape.253
  224.6 13.9 %all-to-all-start.1 = ((f32[128,1,512]{2,1,0:T(1,128)}), f32[128,1,512]{2,1,0:T(1,128)S(1)}, u32[]{:S(2)}, u32[]{:S(2)}) async-start(f32[128,1,512]{2,1,0:T(1,128)} %reshape.253), calls=%async_computation.1 | async-start | bytes 524288 | tf_op jit(solution)/shard_map/all_to_all | solution.py:76
  238.8 11.3 %all-to-all-done.1 = f32[128,1,512]{2,1,0:T(1,128)S(1)} async-done(((f32[128,1,512]{2,1,0:T(1,128)}), f32[128,1,512]{2,1,0:T(1,128)S(1)}, u32[]{:S(2)}, u32[]{:S(2)}) %all-to-all-start.1) | async-done | bytes 262176 | tf_op jit(solution)/shard_map/all_to_all | solution.py:76
  251.3 2.2 reduce
  253.6 0.9 reshape.254
  254.5 1.1 bitcast_reduce_fusion
  256.4 1.1 reshape.225
  257.7 4.0 all_gather.7
  261.7 2.2 gather_fusion
  263.8 4.0 broadcast_in_dim.16
  267.9 32.4 %scatter_fusion = bf16[128,4,4096]{2,1,0:T(4,128)(2,1)} fusion(bf16[128,4,4096]{2,1,0:T(4,128)(2,1)} %broadcast_in_dim.16, s32[128]{0:T(128)S(1)} %fusion.34, bf16[128,4096]{1,0:T(8,128)(2,1)} %gather_fusion), kind=kCustom, calls=%fused_computation.2 | custom fusion | bytes 3146752 | tf_op jit(solution)/shard_map/scatter | solution.py:102
  300.3 110.8 %all_to_all.28 = bf16[128,4,4096]{2,1,0:T(4,128)(2,1)} all-to-all(bf16[128,4,4096]{2,1,0:T(4,128)(2,1)} %scatter_fusion), channel_id=1, replica_groups=mesh['role'=2,'dev'=64,'head'=2] {'role','dev'}, dimensions={0} | all-to-all | bytes 8388608 | tf_op jit(solution)/shard_map/all_to_all | solution.py:104
  411.1 6.9 %reshape.226 = bf16[512,4096]{1,0:T(8,128)(2,1)} reshape(bf16[128,4,4096]{2,1,0:T(4,128)(2,1)} %all_to_all.28) | data formatting | bytes 8388608 | tf_op jit(solution)/shard_map/reshape | solution.py:108
  418.0 5.6 fusion.3
  423.7 3.1 fusion.8
  426.8 1.8 dot_general.32
  428.6 3.3 convolution_convert_fusion
  432.0 3.2 copy.34
  435.2 104.9 %all_to_all.29 = bf16[128,4,4096]{2,1,0:T(4,128)(2,1)S(1)} all-to-all(bf16[128,4,4096]{2,1,0:T(4,128)(2,1)S(1)} %copy.34), channel_id=1, replica_groups=mesh['role'=2,'dev'=64,'head'=2] {'role','dev'}, dimensions={0} | all-to-all | bytes 8388608 | tf_op jit(solution)/shard_map/all_to_all | solution.py:111
  540.1 4.2 copy.35
  545.4 50.9 %reduce-scatter.2.cloned.1.call-done = bf16[128,2,4096]{2,0,1:T(8,128)(2,1)} async-done(((bf16[128,4,4096]{2,0,1:T(8,128)(2,1)}), bf16[128,2,4096]{2,0,1:T(8,128)(2,1)}) %reduce-scatter.2.cloned.1.call-update) | async-done | bytes 2097168 | tf_op jit(solution)/shard_map/reduce_scatter | solution.py:115
  596.3 5.1 copy.36
  601.5 3.3 gather_fusion.1
  604.8 1.5 fusion.13
  (51 shorter events, 6.7 us)
Async XLA Ops:
  6.5 422.1 %copy-start = (bf16[1,384,4096]{2,1,0:T(8,128)(2,1)S(1)}, bf16[1,384,4096]{2,1,0:T(8,128)(2,1)}, u32[]{:S(2)}) copy-start(bf16[1,384,4096]{2,1,0:T(8,128)(2,1)} %param.25) | copy-start | bytes 9437188
  17.7 15.5 %copy-start.5 = (s32[8,8]{1,0:T(8,128)S(1)}, s32[8,8]{1,0:T(8,128)}, u32[]{:S(2)}) copy-start(s32[8,8]{1,0:T(8,128)} %param.26) | copy-start | bytes 772
  17.7 198.2 %all-to-all-start = ((bf16[64,16,4096]{2,1,0:T(8,128)(2,1)}), bf16[64,16,4096]{2,1,0:T(8,128)(2,1)}, u32[]{:S(2)}, u32[]{:S(2)}) async-start(bf16[64,16,4096]{2,1,0:T(8,128)(2,1)} %stack.3), calls=%async_computation | async-start | bytes 16777216 | tf_op jit(solution)/shard_map/all_to_all | solution.py:11
  222.5 34.9 %copy-start.3 = (bf16[8,4096]{1,0:T(8,128)(2,1)S(1)}, bf16[8,4096]{1,0:T(8,128)(2,1)}, u32[]{:S(2)}) copy-start(bf16[8,4096]{1,0:T(8,128)(2,1)} %param.14) | copy-start | bytes 196612
  222.5 35.1 %copy-start.6 = (f32[4096]{0:T(1024)S(1)}, f32[4096]{0:T(1024)}, u32[]{:S(2)}) copy-start(f32[4096]{0:T(1024)} %param.22) | copy-start | bytes 49156
  224.6 25.5 %all-to-all-start.1 = ((f32[128,1,512]{2,1,0:T(1,128)}), f32[128,1,512]{2,1,0:T(1,128)S(1)}, u32[]{:S(2)}, u32[]{:S(2)}) async-start(f32[128,1,512]{2,1,0:T(1,128)} %reshape.253), calls=%async_computation.1 | async-start | bytes 524288 | tf_op jit(solution)/shard_map/all_to_all | solution.py:76
  238.5 357.8 %reduce-scatter.2.cloned.1.call-start = ((), (), s32[]{:S(2)}) async-start(), calls=%async_computation.5 | async-start | bytes 6291456 | tf_op jit(solution)/shard_map/reduce_scatter | solution.py:115
  250.1 0.7 copy-start.2
  418.0 5.6 copy-start.1
  418.0 5.6 copy-start.8
  544.4 0.7 copy-start.7
  545.4 60.9 %copy-start.4 = (bf16[8,4096]{1,0:T(8,128)(2,1)S(1)}, bf16[8,4096]{1,0:T(8,128)(2,1)}, u32[]{:S(2)}) copy-start(bf16[8,4096]{1,0:T(8,128)(2,1)} %param.14) | copy-start | bytes 196612
Sparse Core Ops, SparseCore 0:
  544.5 51.7 reduce-scatter.1
